TPU v7x, 512 devices: a whole 4x4x16 slice. The times are simulated.
512 devices in a mesh: tm: 64 (over y, z), pad: 8 (over x, core).
Axes of the slice: x: 4, y: 4, z: 16, core: 2. Of those that a mesh axis runs over, the one named last changes fastest.
Arguments:
- charge: float32 [8, 32768], P('pad', 'tm'), may hold values from 0.3 to 3
- pad_row: int32 [8, 32768], P('pad', 'tm'), may hold values from 0 to 9
- pad_column: int32 [8, 32768], P('pad', 'tm'), may hold values from 0 to 65
- time_bin: int32 [8, 32768], P('pad', 'tm'), may hold values from 0 to 1023
- slab_owner: int32 [8, 32768, 1], P('pad', 'tm'), may hold values from 0 to 63; in each aligned block of 512 rows (0 to 511, 512 to 1023, ..., all dimensions but the last counted through in order) at most 16 rows name the same one
- block_count: int32 [8, 256], P('pad', 'tm'), may hold values from 1 to 128
- shaping: float32 [1024], replicated, may hold values from 0.02 to 1
- response: float32 [3, 3], replicated, may hold values from 0.05 to 1
Outputs:
- signal: float32 [80, 66, 65536], P('pad', None, 'tm')
Inputs may be any that keep to these rules, and one draw needn't show every extreme that they name: `slab_owner`: among the cluster rows of one device, at most 16 name the same time slab, a bound that some of them reach. Only the first block_count rows of each block of 128 cluster rows hold clusters.
All inputs are finite; a program needn't handle non-finite values.
Results may differ from a plain program's by a relative error of at most 0.0003.
Values sent between devices are 32-bit elements; how exact they have to be, the bound alone decides.
A program may use at most 64 MiB of HBM per device.

v0:
```python
import functools

import jax
import jax.numpy as jnp
from jax import lax
from jax.experimental import pallas as pl
from jax.experimental.pallas import tpu as pltpu
from jax.sharding import PartitionSpec as P

PROWS = 80
PPR = 66
STRIDE = 72
CAP = 16
FIELDS = 4
HALF = FIELDS * CAP
F32 = jnp.float32
BF16 = jnp.bfloat16
LANES = 128
TILE = 256
NT = (((1,), (1,)), ((), ()))


def split(x):
    high = x.astype(BF16)
    return high, (x - high.astype(F32)).astype(BF16)


def route_kernel(last_row, charge_ref, row_ref, column_ref, bin_ref, owner_ref, count_ref, out_ref):
    slabs = out_ref.shape[0]
    clusters = charge_ref.shape[1]
    lane = lax.broadcasted_iota(jnp.int32, (1, clusters), 1)
    limit = jnp.zeros((1, clusters), jnp.int32)
    for block in range(clusters // LANES):
        limit = jnp.where(lane // LANES == block, count_ref[0, block], limit)
    live = lane % LANES < limit
    row = row_ref[...]
    owner = jnp.where(live, owner_ref[...], slabs)
    mine = owner == lax.broadcasted_iota(jnp.int32, (slabs, clusters), 0)
    upper = row == last_row
    lower = row == 0
    middle = jnp.logical_not(jnp.logical_or(upper, lower))
    kinds = [jnp.where(jnp.logical_and(mine, kind), 1.0, 0.0) for kind in (upper, middle, lower)]
    stacked = jnp.concatenate(kinds, axis=0).astype(BF16)
    earlier = (
        lax.broadcasted_iota(jnp.int32, (clusters, clusters), 0)
        < lax.broadcasted_iota(jnp.int32, (clusters, clusters), 1)
    ).astype(F32).astype(BF16)
    ranks = jnp.dot(stacked, earlier, preferred_element_type=F32)
    uppers = jnp.sum(kinds[0], axis=1, keepdims=True)
    places = (
        kinds[0] * ranks[:slabs]
        + kinds[1] * (uppers + ranks[slabs : 2 * slabs])
        + kinds[2] * ((CAP - 1) - ranks[2 * slabs :])
    )
    place = jnp.sum(places, axis=0, keepdims=True).astype(jnp.int32)
    slot = lax.broadcasted_iota(jnp.int32, (CAP, clusters), 0)
    here = place == slot
    fields = (charge_ref[...], row.astype(F32), column_ref[...].astype(F32), bin_ref[...].astype(F32))
    spread_out = jnp.concatenate([jnp.where(here, field, 0.0) for field in fields], axis=0)
    own = lax.dot_general(
        jnp.where(mine, 1.0, 0.0), spread_out, NT, precision=lax.Precision.HIGHEST, preferred_element_type=F32
    )
    slab = lax.broadcasted_iota(jnp.int32, own.shape, 0)
    before = jnp.where(slab == 0, 0.0, pltpu.roll(own, 1, 0))
    out_ref[...] = jnp.concatenate([own, before], axis=1)


def route(charge, row, column, time, owner, count, slabs, last_row):
    return pl.pallas_call(
        functools.partial(route_kernel, last_row),
        out_shape=jax.ShapeDtypeStruct((slabs, 2 * HALF), F32),
        in_specs=[pl.BlockSpec(memory_space=pltpu.VMEM)] * 5 + [pl.BlockSpec(memory_space=pltpu.SMEM)],
        out_specs=pl.BlockSpec(memory_space=pltpu.VMEM),
        name="route",
    )(charge, row, column, time, owner, count)


def zigzag(step, size):
    half = (step + 1) // 2
    away = jnp.where(step % 2 == 0, half, -half)
    return lax.rem(size // 2 + away + size, size)


def exchange_kernel(rows_y, rows_z, send_ref, out_ref, send_sem, recv_sem, side_send, side_recv):
    slabs = send_ref.shape[0]
    groups = lax.axis_size("pad")
    me = lax.axis_index("tm")
    group = lax.axis_index("pad")
    above = lax.rem(group + 1, groups)
    below = lax.rem(group + groups - 1, groups)
    my_y, my_z = me // rows_z, lax.rem(me, rows_z)

    def peer_of(step):
        z = lax.rem(my_z + zigzag(step // rows_y, rows_z), rows_z)
        y = lax.rem(my_y + zigzag(lax.rem(step, rows_y), rows_y), rows_y)
        return y * rows_z + z

    barrier = pltpu.get_barrier_semaphore()

    def greet(step, carry):
        pl.semaphore_signal(
            barrier, inc=1, device_id=(peer_of(step), group), device_id_type=pl.DeviceIdType.MESH
        )
        return carry

    lax.fori_loop(0, slabs - 1, greet, 0)
    for side in (above, below):
        pl.semaphore_signal(barrier, inc=1, device_id=(me, side), device_id_type=pl.DeviceIdType.MESH)
    out_ref[1, pl.ds(me, 1)] = send_ref[pl.ds(me, 1)]
    pl.semaphore_wait(barrier, slabs + 1)

    def send(step, carry):
        peer = peer_of(step)
        pltpu.make_async_remote_copy(
            src_ref=send_ref.at[pl.ds(peer, 1)],
            dst_ref=out_ref.at[1, pl.ds(me, 1)],
            send_sem=send_sem,
            recv_sem=recv_sem,
            device_id=(peer, group),
            device_id_type=pl.DeviceIdType.MESH,
        ).start()
        return carry

    lax.fori_loop(0, slabs - 1, send, 0)
    whole = pltpu.make_async_copy(
        send_ref.at[pl.ds(0, slabs - 1)], out_ref.at[1, pl.ds(0, slabs - 1)], recv_sem
    )
    whole.wait()
    copies = []
    for index, (side, place) in enumerate(((above, 0), (below, 2))):
        copies.append(
            pltpu.make_async_remote_copy(
                src_ref=out_ref.at[1],
                dst_ref=out_ref.at[place],
                send_sem=side_send.at[index],
                recv_sem=side_recv.at[index],
                device_id=(me, side),
                device_id_type=pl.DeviceIdType.MESH,
            )
        )
        copies[-1].start()
    pltpu.make_async_copy(
        send_ref.at[pl.ds(0, slabs - 1)], out_ref.at[1, pl.ds(0, slabs - 1)], send_sem
    ).wait()
    for copy in copies:
        copy.wait()

    @pl.when(group == 0)
    def _():
        out_ref[0] = jnp.zeros(out_ref.shape[1:], F32)

    @pl.when(group == groups - 1)
    def _():
        out_ref[2] = jnp.zeros(out_ref.shape[1:], F32)


def exchange(rows, rows_y):
    slabs, width = rows.shape
    return pl.pallas_call(
        functools.partial(exchange_kernel, rows_y, slabs // rows_y),
        out_shape=jax.ShapeDtypeStruct((3, slabs, width), F32),
        in_specs=[pl.BlockSpec(memory_space=pltpu.VMEM)],
        out_specs=pl.BlockSpec(memory_space=pltpu.VMEM),
        scratch_shapes=[
            pltpu.SemaphoreType.DMA,
            pltpu.SemaphoreType.DMA,
            pltpu.SemaphoreType.DMA((2,)),
            pltpu.SemaphoreType.DMA((2,)),
        ],
        compiler_params=pltpu.CompilerParams(collective_id=0, has_side_effects=True),
        name="exchange",
    )(rows)


def digitize_kernel(
    row_count, bins, recv_ref, shaping_ref, response_ref, out_ref,
    high, low, table_high, table_low, wide, hits, parts, shaped, edges, held, columns,
):
    slabs = recv_ref.shape[1]
    step = pl.program_id(0)
    cells = row_count * STRIDE
    slots = slabs * CAP
    pairs = CAP // 2
    chunk = 4 * slabs

    def sides(which):
        flipped = jnp.transpose(recv_ref[which])
        return [
            [
                jnp.concatenate(
                    [
                        flipped[HALF * slab + CAP * field : HALF * slab + CAP * field + pairs],
                        flipped[HALF * slab + CAP * field + pairs : HALF * slab + CAP * (field + 1)],
                    ],
                    axis=1,
                )
                for field in range(FIELDS)
            ]
            for slab in range(2)
        ]

    def hit_rows(which, slab, slot):
        at = HALF * slab + CAP * 3 + (slot % 2) * pairs + slot // 2
        column = recv_ref[which, :, at : at + 1].astype(jnp.int32)
        moment = lax.broadcasted_iota(jnp.int32, (slabs, bins), 1)
        return jnp.where(moment == column, 1.0, 0.0).astype(BF16)

    @pl.when(step == 0)
    def _():
        lags = shaping_ref.shape[1]
        line = jnp.concatenate(
            [jnp.zeros((1, TILE), F32), shaping_ref[...], jnp.zeros((1, TILE), F32)], axis=1
        )
        rolled = pltpu.roll(
            jnp.broadcast_to(line, (TILE, lags + 2 * TILE)), 0, 1, stride=1, stride_axis=0
        )
        top, rest = split(rolled)
        for block in range(lags // TILE + 1):
            at = lags + TILE - TILE * block
            table_high[TILE * block : TILE * (block + 1)] = top[:, at : at + TILE]
            table_low[TILE * block : TILE * (block + 1)] = rest[:, at : at + TILE]

        own = sides(1)
        pad = lax.broadcasted_iota(jnp.int32, (STRIDE, 2 * slabs), 0)
        for slab in range(2):
            charge, row, column, _ = own[slab]
            for pair in range(pairs):
                there = pad == column[pair : pair + 1].astype(jnp.int32)
                lanes = slice(2 * slabs * pair, 2 * slabs * (pair + 1))
                for lead in range(0, row_count, 2):
                    both = []
                    for r in (lead, lead + 1):
                        value = jnp.where(row[pair : pair + 1] == float(r), charge[pair : pair + 1], 0.0)
                        both.append(jnp.where(there, value, 0.0))
                    top, rest = split(jnp.concatenate(both, axis=0))
                    at = lead * STRIDE
                    wide[at : at + 2 * STRIDE, lanes] = top
                    wide[cells + at : cells + at + 2 * STRIDE, lanes] = rest
            for slot in range(CAP):
                hits[slabs * slot : slabs * (slot + 1)] = hit_rows(1, slab, slot)
            base = bins * (1 - slab)

            def lay(block, carry):
                at = pl.multiple_of(block * TILE, TILE)
                both = jnp.dot(wide[...], hits[:, pl.ds(at, TILE)], preferred_element_type=F32)
                top, rest = split(both[:cells] + both[cells:])
                to = pl.multiple_of(base + at, TILE)
                high[STRIDE : STRIDE + cells, pl.ds(to, TILE)] = top
                low[STRIDE : STRIDE + cells, pl.ds(to, TILE)] = rest
                return carry

            lax.fori_loop(0, bins // TILE, lay, 0)

        held[...] = jnp.zeros(held.shape, F32)
        needed = jnp.zeros((), F32)
        for index, which in enumerate((0, 2)):
            fields = sides(which)
            edge = float(row_count - 1) if which == 0 else 0.0
            place = 2 * lax.broadcasted_iota(jnp.int32, (pairs, 2 * slabs), 0) + (
                lax.broadcasted_iota(jnp.int32, (pairs, 2 * slabs), 1) // slabs
            )
            depth = (place if which == 0 else CAP - 1 - place) + 1
            for slab in range(2):
                charge, row, column, _ = fields[slab]
                kept = jnp.where(row == edge, charge, 0.0)
                needed = jnp.maximum(needed, jnp.max(jnp.where(kept != 0.0, depth, 0).astype(F32)))
                edges[index, slab, 0] = kept
                edges[index, slab, 1] = column
        chunks = (needed.astype(jnp.int32) + 3) // 4
        for number in range(CAP // 4):

            @pl.when(number < chunks)
            def _():
                for index, which in enumerate((0, 2)):
                    first = 4 * number if which == 0 else CAP - 4 - 4 * number
                    for slab in range(2):
                        weights = []
                        for pair in (first // 2, first // 2 + 1):
                            there = pad == edges[index, slab, 1, pair : pair + 1].astype(jnp.int32)
                            weights.append(jnp.where(there, edges[index, slab, 0, pair : pair + 1], 0.0))
                        top = jnp.concatenate(weights, axis=1)
                        rest = top - top.astype(BF16).astype(F32)
                        left = jnp.concatenate([top, rest], axis=0).astype(BF16)
                        right = jnp.concatenate(
                            [hit_rows(which, slab, first + k) for k in range(4)], axis=0
                        )
                        both = jnp.dot(left, right, preferred_element_type=F32)
                        at = bins * (1 - slab)
                        held[index, :, at : at + bins] += both[:STRIDE] + both[STRIDE:]

        for index, at in enumerate((0, STRIDE + cells)):
            top, rest = split(held[index])
            high[at : at + STRIDE] = top
            low[at : at + STRIDE] = rest

    start = pl.multiple_of(step * TILE, TILE)
    depth = table_high.shape[0]
    upper = high[:, pl.ds(start, depth)]
    shaped[...] = (
        jnp.dot(upper, table_high[...], preferred_element_type=F32)
        + jnp.dot(upper, table_low[...], preferred_element_type=F32)
        + jnp.dot(low[:, pl.ds(start, depth)], table_high[...], preferred_element_type=F32)
    )

    def spread(r, carry):
        at = pl.multiple_of(r * STRIDE, 8)
        near = [shaped[pl.ds(pl.multiple_of(at + STRIDE * a, 8), STRIDE)] for a in range(3)]
        sums = []
        for b in range(3):
            sums.append(
                response_ref[0, b] * near[0] + response_ref[1, b] * near[1] + response_ref[2, b] * near[2]
            )
        total = sums[1] + pltpu.roll(sums[0], 1, 0) + pltpu.roll(sums[2], STRIDE - 1, 0)
        out_ref[r] = total[:PPR]
        return carry

    lax.fori_loop(0, row_count, spread, 0)


def digitize(recv, shaping, response, row_count, bins):
    slabs = recv.shape[1]
    lags = shaping.shape[1]
    cells = row_count * STRIDE
    grid_rows = cells + 2 * STRIDE
    return pl.pallas_call(
        functools.partial(digitize_kernel, row_count, bins),
        out_shape=jax.ShapeDtypeStruct((row_count, PPR, bins), F32),
        grid=(bins // TILE,),
        in_specs=[
            pl.BlockSpec(memory_space=pltpu.VMEM),
            pl.BlockSpec(memory_space=pltpu.VMEM),
            pl.BlockSpec(memory_space=pltpu.SMEM),
        ],
        out_specs=pl.BlockSpec((row_count, PPR, TILE), lambda i: (0, 0, i)),
        scratch_shapes=[
            pltpu.VMEM((grid_rows, 2 * bins), BF16),
            pltpu.VMEM((grid_rows, 2 * bins), BF16),
            pltpu.VMEM((lags + TILE, TILE), BF16),
            pltpu.VMEM((lags + TILE, TILE), BF16),
            pltpu.VMEM((2 * cells, CAP * slabs), BF16),
            pltpu.VMEM((CAP * slabs, bins), BF16),
            pltpu.VMEM((8, 128), F32),
            pltpu.VMEM((grid_rows, TILE), F32),
            pltpu.VMEM((2, 2, 2, CAP // 2, 2 * slabs), F32),
            pltpu.VMEM((2, STRIDE, 2 * bins), F32),
            pltpu.VMEM((8, 128), F32),
        ],
        compiler_params=pltpu.CompilerParams(
            dimension_semantics=("arbitrary",), vmem_limit_bytes=60 * 1024 * 1024
        ),
        name="digitize",
    )(recv, shaping, response)


def solution(mesh):
    slabs, groups = mesh.shape["tm"], mesh.shape["pad"]
    row_count = PROWS // groups
    bins = 1024
    rows_y = 4 if slabs % 4 == 0 else 1

    def body(charge, pad_row, pad_column, time_bin, slab_owner, block_count, shaping, response):
        owner = slab_owner.reshape(1, slab_owner.shape[1])
        rows = route(charge, pad_row, pad_column, time_bin, owner, block_count, slabs, row_count - 1)
        received = exchange(rows, rows_y)
        return digitize(received, shaping.reshape(1, shaping.shape[0]), response, row_count, bins)

    in_specs = (P("pad", "tm"),) * 4 + (P("pad", "tm", None), P("pad", "tm"), P(), P())
    return jax.shard_map(
        body, mesh=mesh, in_specs=in_specs, out_specs=P("pad", None, "tm"), check_vma=False
    )
```

profile of v0, /device:TPU:1, one launch (start us, length us, event | category | flops | bytes accessed | tf_op | source)
XLA Modules:
  0.0 54.3 jit_solution(10704198717798384882)
XLA Ops:
  0.0 2.1 %route.1.send_ref = f32[64,128]{1,0:T(8,128)} custom-call(f32[1,512]{1,0:T(1,128)} %charge_ref.1, s32[1,512]{1,0:T(1,128)} %row_ref.1, s32[1,512]{1,0:T(1,128)} %column_ref.1, s32[1,512]{1,0:T(1,128)} %bin_ref.1, s32[1,512]{1,0:T(1,128)} %bitcast.3, s32[1,4]{1,0:T(1,128)} %count_ref.1), custom_call_target="tpu_custom_call" | custom-call | tf_op jit(solution)/shard_map/route/pallas_call | solution.py:69
  2.1 28.8 %exchange.1.recv_ref = f32[3,64,128]{2,1,0:T(8,128)} custom-call(f32[64,128]{1,0:T(8,128)} %route.1.send_ref), custom_call_target="tpu_custom_call" | custom-call | tf_op jit(solution)/shard_map/exchange/pallas_call | solution.py:159
  30.9 23.4 %digitize.1 = f32[10,66,1024]{2,1,0:T(8,128)} custom-call(f32[3,64,128]{2,1,0:T(8,128)} %exchange.1.recv_ref, f32[1,1024]{1,0:T(1,128)} %bitcast.2, f32[3,3]{1,0:T(4,128)} %response_ref.1), custom_call_target="tpu_custom_call" | custom-call | tf_op jit(solution)/shard_map/digitize/pallas_call | solution.py:325
where the time goes:
time: 54.7 us; the launch traced here: 54.3 us
  Pallas kernels  54.3 us (99%)
    pallas_call x1, Pallas kernels, exchange(): pl.pallas_call(functools.partial(exchange_kernel, rows_y, slabs // rows_y...  28.8 us
    pallas_call x1, Pallas kernels, digitize(): pl.pallas_call(functools.partial(digitize_kernel, row_count, bins), out_s...  23.4 us
    pallas_call x1, Pallas kernels, route(): pl.pallas_call(functools.partial(route_kernel, last_row), out_shape=jax.S...  2.07 us

commit v1 on v0

v1 whole, which is shorter than its diff:
```python
import functools

import jax
import jax.numpy as jnp
from jax import lax
from jax.experimental import pallas as pl
from jax.experimental.pallas import tpu as pltpu
from jax.sharding import PartitionSpec as P

PROWS = 80
PPR = 66
STRIDE = 72
CAP = 16
FIELDS = 4
HALF = FIELDS * CAP
F32 = jnp.float32
BF16 = jnp.bfloat16
LANES = 128
TILE = 256
NT = (((1,), (1,)), ((), ()))


def split(x):
    high = x.astype(BF16)
    return high, (x - high.astype(F32)).astype(BF16)


def route_rows(last_row, slabs, charge, row, column, moment, owner, count):
    clusters = charge.shape[1]
    lane = lax.broadcasted_iota(jnp.int32, (1, clusters), 1)
    limit = jnp.zeros((1, clusters), jnp.int32)
    for block in range(clusters // LANES):
        limit = jnp.where(lane // LANES == block, count[:, block : block + 1], limit)
    live = lane % LANES < limit
    owner = jnp.where(live, owner, slabs)
    mine = owner == lax.broadcasted_iota(jnp.int32, (slabs, clusters), 0)
    upper = row == last_row
    lower = row == 0
    middle = jnp.logical_not(jnp.logical_or(upper, lower))
    kinds = [jnp.where(jnp.logical_and(mine, kind), 1.0, 0.0) for kind in (upper, middle, lower)]
    stacked = jnp.concatenate(kinds, axis=0).astype(BF16)
    earlier = (
        lax.broadcasted_iota(jnp.int32, (clusters, clusters), 0)
        < lax.broadcasted_iota(jnp.int32, (clusters, clusters), 1)
    ).astype(F32).astype(BF16)
    ranks = jnp.dot(stacked, earlier, preferred_element_type=F32)
    uppers = jnp.sum(kinds[0], axis=1, keepdims=True)
    places = (
        kinds[0] * ranks[:slabs]
        + kinds[1] * (uppers + ranks[slabs : 2 * slabs])
        + kinds[2] * ((CAP - 1) - ranks[2 * slabs :])
    )
    place = jnp.sum(places, axis=0, keepdims=True)
    slot = lax.broadcasted_iota(jnp.int32, (CAP, clusters), 0)
    half = CAP // 2
    here = place == (2 * (slot % half) + slot // half).astype(F32)
    fields = (charge, row.astype(F32), column.astype(F32), moment.astype(F32))
    spread_out = jnp.concatenate([jnp.where(here, field, 0.0) for field in fields], axis=0)
    own = lax.dot_general(
        jnp.where(mine, 1.0, 0.0), spread_out, NT, precision=lax.Precision.HIGHEST, preferred_element_type=F32
    )
    slab = lax.broadcasted_iota(jnp.int32, own.shape, 0)
    before = jnp.where(slab == 0, 0.0, pltpu.roll(own, 1, 0))
    return jnp.concatenate([own, before], axis=1)


def lag_table(shaping):
    lags = shaping.shape[1]
    line = jnp.concatenate([jnp.zeros((1, TILE), F32), shaping, jnp.zeros((1, TILE), F32)], axis=1)
    rolled = pltpu.roll(
        jnp.broadcast_to(line, (TILE, lags + 2 * TILE)), 0, 1, stride=1, stride_axis=0
    )
    blocks = []
    for block in range(lags // TILE + 1):
        at = lags + TILE - TILE * block
        blocks.append(rolled[:, at : at + TILE])
    return blocks


def zigzag(step, size):
    half = (step + 1) // 2
    away = jnp.where(step % 2 == 0, half, -half)
    return lax.rem(size // 2 + away + size, size)


def exchange_kernel(
    last_row, rows_y, rows_z, charge_ref, row_ref, column_ref, bin_ref, owner_ref, count_ref, shaping_ref,
    out_ref, table_ref, floats, ints, counts, line, rows, table, load_sem, send_sem, recv_sem, side_send, side_recv,
):
    slabs = rows.shape[0]
    groups = lax.axis_size("pad")
    me = lax.axis_index("tm")
    group = lax.axis_index("pad")
    above = lax.rem(group + 1, groups)
    below = lax.rem(group + groups - 1, groups)
    my_y, my_z = me // rows_z, lax.rem(me, rows_z)
    loads = [
        pltpu.make_async_copy(source, target, load_sem.at[index])
        for index, (source, target) in enumerate(
            (
                (charge_ref, floats),
                (row_ref, ints.at[0]),
                (column_ref, ints.at[1]),
                (bin_ref, ints.at[2]),
                (owner_ref, ints.at[3]),
                (count_ref, counts),
                (shaping_ref, line),
            )
        )
    ]
    for load in loads:
        load.start()

    def peer_of(step):
        z = lax.rem(my_z + zigzag(step // rows_y, rows_z), rows_z)
        y = lax.rem(my_y + zigzag(lax.rem(step, rows_y), rows_y), rows_y)
        return y * rows_z + z

    barrier = pltpu.get_barrier_semaphore()

    def greet(step, carry):
        pl.semaphore_signal(
            barrier, inc=1, device_id=(peer_of(step), group), device_id_type=pl.DeviceIdType.MESH
        )
        return carry

    lax.fori_loop(0, slabs - 1, greet, 0)
    for side in (above, below):
        pl.semaphore_signal(barrier, inc=1, device_id=(me, side), device_id_type=pl.DeviceIdType.MESH)
    for load in loads:
        load.wait()
    rows[...] = route_rows(
        last_row, slabs, floats[...], ints[0], ints[1], ints[2], ints[3], counts[...]
    )
    for index, block in enumerate(lag_table(line[...])):
        high, low = split(block)
        table[0, TILE * index : TILE * (index + 1)] = high
        table[1, TILE * index : TILE * (index + 1)] = low
    store = pltpu.make_async_copy(table, table_ref, load_sem.at[0])
    store.start()
    out_ref[1, pl.ds(me, 1)] = rows[pl.ds(me, 1)]
    pl.semaphore_wait(barrier, slabs + 1)

    def send(step, carry):
        peer = peer_of(step)
        pltpu.make_async_remote_copy(
            src_ref=rows.at[pl.ds(peer, 1)],
            dst_ref=out_ref.at[1, pl.ds(me, 1)],
            send_sem=send_sem,
            recv_sem=recv_sem,
            device_id=(peer, group),
            device_id_type=pl.DeviceIdType.MESH,
        ).start()
        return carry

    lax.fori_loop(0, slabs - 1, send, 0)
    some = rows.at[pl.ds(0, slabs - 1)]
    pltpu.make_async_copy(some, out_ref.at[1, pl.ds(0, slabs - 1)], recv_sem).wait()
    copies = []
    for index, (side, place) in enumerate(((above, 0), (below, 2))):
        copies.append(
            pltpu.make_async_remote_copy(
                src_ref=out_ref.at[1],
                dst_ref=out_ref.at[place],
                send_sem=side_send.at[index],
                recv_sem=side_recv.at[index],
                device_id=(me, side),
                device_id_type=pl.DeviceIdType.MESH,
            )
        )
        copies[-1].start()
    pltpu.make_async_copy(some, out_ref.at[1, pl.ds(0, slabs - 1)], send_sem).wait()
    store.wait()
    for copy in copies:
        copy.wait()

    @pl.when(group == 0)
    def _():
        out_ref[0] = jnp.zeros(out_ref.shape[1:], F32)

    @pl.when(group == groups - 1)
    def _():
        out_ref[2] = jnp.zeros(out_ref.shape[1:], F32)


def exchange(charge, row, column, moment, owner, count, shaping, slabs, last_row, rows_y):
    clusters, lags = charge.shape[1], shaping.shape[1]
    return pl.pallas_call(
        functools.partial(exchange_kernel, last_row, rows_y, slabs // rows_y),
        out_shape=(
            jax.ShapeDtypeStruct((3, slabs, 2 * HALF), F32),
            jax.ShapeDtypeStruct((2, lags + TILE, TILE), BF16),
        ),
        in_specs=[pl.BlockSpec(memory_space=pl.ANY)] * 7,
        out_specs=(pl.BlockSpec(memory_space=pltpu.VMEM), pl.BlockSpec(memory_space=pl.ANY)),
        scratch_shapes=[
            pltpu.VMEM((1, clusters), F32),
            pltpu.VMEM((4, 1, clusters), jnp.int32),
            pltpu.VMEM(count.shape, jnp.int32),
            pltpu.VMEM((1, lags), F32),
            pltpu.VMEM((slabs, 2 * HALF), F32),
            pltpu.VMEM((2, lags + TILE, TILE), BF16),
            pltpu.SemaphoreType.DMA((7,)),
            pltpu.SemaphoreType.DMA,
            pltpu.SemaphoreType.DMA,
            pltpu.SemaphoreType.DMA((2,)),
            pltpu.SemaphoreType.DMA((2,)),
        ],
        compiler_params=pltpu.CompilerParams(collective_id=0, has_side_effects=True),
        name="exchange",
    )(charge, row, column, moment, owner, count, shaping)


def digitize_kernel(
    row_count, bins, recv_ref, table_ref, response_ref, out_ref,
    high, low, table, wides, hits, shaped, edges, held, staged, table_sem, out_sem,
):
    load = pltpu.make_async_copy(table_ref, table, table_sem)
    load.start()
    slabs = recv_ref.shape[1]
    cells = row_count * STRIDE
    pairs = CAP // 2

    def sides(which):
        flipped = jnp.transpose(recv_ref[which])
        return [
            [
                jnp.concatenate(
                    [
                        flipped[HALF * slab + CAP * field : HALF * slab + CAP * field + pairs],
                        flipped[HALF * slab + CAP * field + pairs : HALF * slab + CAP * (field + 1)],
                    ],
                    axis=1,
                )
                for field in range(FIELDS)
            ]
            for slab in range(2)
        ]

    def hit_rows(which, slab, slot):
        at = HALF * slab + CAP * 3 + (slot % 2) * pairs + slot // 2
        column = recv_ref[which, :, at : at + 1].astype(jnp.int32)
        moment = lax.broadcasted_iota(jnp.int32, (slabs, bins), 1)
        return jnp.where(moment == column, 1.0, 0.0).astype(BF16)

    own = sides(1)
    pad = lax.broadcasted_iota(jnp.int32, (STRIDE, 2 * slabs), 0)
    for slab in range(2):
        charge, row, column, _ = own[slab]
        wide = wides.at[slab]
        for pair in range(pairs):
            there = pad == column[pair : pair + 1].astype(jnp.int32)
            lanes = slice(2 * slabs * pair, 2 * slabs * (pair + 1))
            for lead in range(0, row_count, 2):
                both = []
                for r in (lead, lead + 1):
                    value = jnp.where(row[pair : pair + 1] == float(r), charge[pair : pair + 1], 0.0)
                    both.append(jnp.where(there, value, 0.0))
                top, rest = split(jnp.concatenate(both, axis=0))
                at = lead * STRIDE
                wide[at : at + 2 * STRIDE, lanes] = top
                wide[cells + at : cells + at + 2 * STRIDE, lanes] = rest
        for slot in range(CAP):
            hits[slab, slabs * slot : slabs * (slot + 1)] = hit_rows(1, slab, slot)
        base = bins * (1 - slab)
        both = jnp.dot(wide[...], hits[slab], preferred_element_type=F32)
        top, rest = split(both[:cells] + both[cells:])
        high[STRIDE : STRIDE + cells, base : base + bins] = top
        low[STRIDE : STRIDE + cells, base : base + bins] = rest

    held[...] = jnp.zeros(held.shape, F32)
    needed = jnp.zeros((), F32)
    for index, which in enumerate((0, 2)):
        fields = sides(which)
        edge = float(row_count - 1) if which == 0 else 0.0
        place = 2 * lax.broadcasted_iota(jnp.int32, (pairs, 2 * slabs), 0) + (
            lax.broadcasted_iota(jnp.int32, (pairs, 2 * slabs), 1) // slabs
        )
        depth = (place if which == 0 else CAP - 1 - place) + 1
        for slab in range(2):
            charge, row, column, _ = fields[slab]
            kept = jnp.where(row == edge, charge, 0.0)
            needed = jnp.maximum(needed, jnp.max(jnp.where(kept != 0.0, depth, 0).astype(F32)))
            edges[index, slab, 0] = kept
            edges[index, slab, 1] = column
    chunks = (needed.astype(jnp.int32) + 3) // 4
    for number in range(CAP // 4):

        @pl.when(number < chunks)
        def _():
            for index, which in enumerate((0, 2)):
                first = 4 * number if which == 0 else CAP - 4 - 4 * number
                for slab in range(2):
                    weights = []
                    for pair in (first // 2, first // 2 + 1):
                        there = pad == edges[index, slab, 1, pair : pair + 1].astype(jnp.int32)
                        weights.append(jnp.where(there, edges[index, slab, 0, pair : pair + 1], 0.0))
                    top = jnp.concatenate(weights, axis=1)
                    rest = top - top.astype(BF16).astype(F32)
                    left = jnp.concatenate([top, rest], axis=0).astype(BF16)
                    right = jnp.concatenate(
                        [hit_rows(which, slab, first + k) for k in range(4)], axis=0
                    )
                    both = jnp.dot(left, right, preferred_element_type=F32)
                    at = bins * (1 - slab)
                    held[index, :, at : at + bins] += both[:STRIDE] + both[STRIDE:]

    for index, at in enumerate((0, STRIDE + cells)):
        top, rest = split(held[index])
        high[at : at + STRIDE] = top
        low[at : at + STRIDE] = rest

    load.wait()
    depth = table.shape[1]
    steps = bins // TILE
    copies = []
    for step in range(steps + 1):
        if step < steps:
            upper = high[:, TILE * step : TILE * step + depth]
            shaped[step % 2] = (
                jnp.dot(upper, table[0], preferred_element_type=F32)
                + jnp.dot(upper, table[1], preferred_element_type=F32)
                + jnp.dot(
                    low[:, TILE * step : TILE * step + depth], table[0], preferred_element_type=F32
                )
            )
        if step > 0:
            done = step - 1
            if done >= 2:
                copies[done - 2].wait()
            for r in range(row_count):
                near = [shaped[done % 2, STRIDE * (r + a) : STRIDE * (r + a + 1)] for a in range(3)]
                sums = []
                for b in range(3):
                    sums.append(
                        response_ref[0, b] * near[0] + response_ref[1, b] * near[1] + response_ref[2, b] * near[2]
                    )
                total = sums[1] + pltpu.roll(sums[0], 1, 0) + pltpu.roll(sums[2], STRIDE - 1, 0)
                staged[done % 2, r] = total[:PPR]
            copies.append(
                pltpu.make_async_copy(
                    staged.at[done % 2],
                    out_ref.at[:, :, pl.ds(TILE * done, TILE)],
                    out_sem.at[done % 2],
                )
            )
            copies[-1].start()
    for copy in copies[-2:]:
        copy.wait()


def digitize(recv, table, response, row_count, bins):
    slabs = recv.shape[1]
    cells = row_count * STRIDE
    grid_rows = cells + 2 * STRIDE
    return pl.pallas_call(
        functools.partial(digitize_kernel, row_count, bins),
        out_shape=jax.ShapeDtypeStruct((row_count, PPR, bins), F32),
        in_specs=[
            pl.BlockSpec(memory_space=pltpu.VMEM),
            pl.BlockSpec(memory_space=pl.ANY),
            pl.BlockSpec(memory_space=pltpu.SMEM),
        ],
        out_specs=pl.BlockSpec(memory_space=pl.ANY),
        scratch_shapes=[
            pltpu.VMEM((grid_rows, 2 * bins), BF16),
            pltpu.VMEM((grid_rows, 2 * bins), BF16),
            pltpu.VMEM(table.shape, BF16),
            pltpu.VMEM((2, 2 * cells, CAP * slabs), BF16),
            pltpu.VMEM((2, CAP * slabs, bins), BF16),
            pltpu.VMEM((2, grid_rows, TILE), F32),
            pltpu.VMEM((2, 2, 2, CAP // 2, 2 * slabs), F32),
            pltpu.VMEM((2, STRIDE, 2 * bins), F32),
            pltpu.VMEM((2, row_count, PPR, TILE), F32),
            pltpu.SemaphoreType.DMA,
            pltpu.SemaphoreType.DMA((2,)),
        ],
        compiler_params=pltpu.CompilerParams(vmem_limit_bytes=60 * 1024 * 1024),
        name="digitize",
    )(recv, table, response)


def solution(mesh):
    slabs, groups = mesh.shape["tm"], mesh.shape["pad"]
    row_count = PROWS // groups
    bins = 1024
    rows_y = 4 if slabs % 4 == 0 else 1

    def body(charge, pad_row, pad_column, time_bin, slab_owner, block_count, shaping, response):
        owner = slab_owner.reshape(1, slab_owner.shape[1])
        line = shaping.reshape(1, shaping.shape[0])
        received, table = exchange(
            charge, pad_row, pad_column, time_bin, owner, block_count, line, slabs, row_count - 1, rows_y
        )
        return digitize(received, table, response, row_count, bins)

    in_specs = (P("pad", "tm"),) * 4 + (P("pad", "tm", None), P("pad", "tm"), P(), P())
    return jax.shard_map(
        body, mesh=mesh, in_specs=in_specs, out_specs=P("pad", None, "tm"), check_vma=False
    )
```

time: 54.7 us -> 48 us (0.88)
  Pallas kernels: 54.3 us -> 47.7 us
    pallas_call x1, Pallas kernels: 23.4 us -> 19.1 us  [digitize(): pl.pallas_call(functools.partial(digitize_kernel, row_count, bins), out_s...]
    pallas_call x2 -> x1, Pallas kernels: 30.9 us -> 28.6 us  [exchange(): pl.pallas_call(functools.partial(exchange_kernel, last_row, rows_y, slabs...]
where the time goes in v1:
time: 48 us; the launch traced here: 47.9 us
  Pallas kernels  47.7 us (99%)
    pallas_call x1, Pallas kernels, exchange(): pl.pallas_call(functools.partial(exchange_kernel, last_row, rows_y, slabs...  28.6 us
    pallas_call x1, Pallas kernels, digitize(): pl.pallas_call(functools.partial(digitize_kernel, row_count, bins), out_s...  19.1 us

profile of v1, /device:TPU:1, one launch (start us, length us, event | category | flops | bytes accessed | tf_op | source)
XLA Modules:
  0.0 47.9 jit_solution(7416268582169875194)
XLA Ops:
  0.0 28.6 %exchange.1 = (f32[3,64,128]{2,1,0:T(8,128)}, bf16[2,1280,256]{2,1,0:T(8,128)(2,1)}) custom-call(f32[1,512]{1,0:T(1,128)} %charge_ref.1, s32[1,512]{1,0:T(1,128)} %row_ref.1, s32[1,512]{1,0:T(1,128)} %column_ref.1, s32[1,512]{1,0:T(1,128)} %bin_ref.1, s32[1,512]{1,0:T(1,128)} %bitcast.3, s32[1,4]{1,0:T(1,128)} %count_ref.1, f32[1,1024]{1,0:T(1,128)} %bitcast.2), custom_call_target="tpu_custom_call" | custom-call | tf_op jit(solution)/shard_map/exchange/pallas_call | solution.py:188
  28.6 19.1 %digitize.1 = f32[10,66,1024]{2,1,0:T(8,128)} custom-call(f32[3,64,128]{2,1,0:T(8,128)} %get-tuple-element.7.recv_ref, bf16[2,1280,256]{2,1,0:T(8,128)(2,1)} %get-tuple-element.8.table_ref, f32[3,3]{1,0:T(4,128)} %response_ref.1), custom_call_target="tpu_custom_call" | custom-call | tf_op jit(solution)/shard_map/digitize/pallas_call | solution.py:356

commit v2 on v1

--- a/solution.py
+++ b/solution.py
@@ -15,6 +15,13 @@
 HALF = FIELDS * CAP
 F32 = jnp.float32
 BF16 = jnp.bfloat16
+F8 = jnp.float8_e4m3fn
+GRID, GRID_LOW = 2.0**-3, 2.0**8
+TABLE_HIGH, TABLE_LOW = 2.0**7, 2.0**15
+CHARGE_LOW = 2.0**17
+UPPER = 448
+MAIN = 12
+FINE = 2.0**-15
 LANES = 128
 TILE = 256
 NT = (((1,), (1,)), ((), ()))
@@ -34,21 +41,28 @@
     live = lane % LANES < limit
     owner = jnp.where(live, owner, slabs)
     mine = owner == lax.broadcasted_iota(jnp.int32, (slabs, clusters), 0)
-    upper = row == last_row
-    lower = row == 0
-    middle = jnp.logical_not(jnp.logical_or(upper, lower))
-    kinds = [jnp.where(jnp.logical_and(mine, kind), 1.0, 0.0) for kind in (upper, middle, lower)]
+    middle = (last_row + 1) // 2
+    order = (
+        row == last_row,
+        jnp.logical_and(row >= middle, row < last_row),
+        jnp.logical_and(row < middle, row > 0),
+        row == 0,
+    )
+    kinds = [jnp.where(jnp.logical_and(mine, kind), 1.0, 0.0) for kind in order]
     stacked = jnp.concatenate(kinds, axis=0).astype(BF16)
     earlier = (
         lax.broadcasted_iota(jnp.int32, (clusters, clusters), 0)
         < lax.broadcasted_iota(jnp.int32, (clusters, clusters), 1)
     ).astype(F32).astype(BF16)
     ranks = jnp.dot(stacked, earlier, preferred_element_type=F32)
-    uppers = jnp.sum(kinds[0], axis=1, keepdims=True)
+    ranks = [ranks[slabs * k : slabs * (k + 1)] for k in range(4)]
+    firsts = jnp.sum(kinds[0], axis=1, keepdims=True)
+    lasts = jnp.sum(kinds[3], axis=1, keepdims=True)
     places = (
-        kinds[0] * ranks[:slabs]
-        + kinds[1] * (uppers + ranks[slabs : 2 * slabs])
-        + kinds[2] * ((CAP - 1) - ranks[2 * slabs :])
+        kinds[0] * ranks[0]
+        + kinds[1] * (firsts + ranks[1])
+        + kinds[2] * ((CAP - 1) - lasts - ranks[2])
+        + kinds[3] * ((CAP - 1) - ranks[3])
     )
     place = jnp.sum(places, axis=0, keepdims=True)
     slot = lax.broadcasted_iota(jnp.int32, (CAP, clusters), 0)
@@ -75,6 +89,10 @@
         at = lags + TILE - TILE * block
         blocks.append(rolled[:, at : at + TILE])
     return blocks
+
+
+def in_hbm(x):
+    return pltpu.with_memory_space_constraint(x, pltpu.HBM)
 
 
 def zigzag(step, size):
@@ -191,7 +209,7 @@
             jax.ShapeDtypeStruct((3, slabs, 2 * HALF), F32),
             jax.ShapeDtypeStruct((2, lags + TILE, TILE), BF16),
         ),
-        in_specs=[pl.BlockSpec(memory_space=pl.ANY)] * 7,
+        in_specs=[pl.BlockSpec(memory_space=pltpu.HBM)] * 7,
         out_specs=(pl.BlockSpec(memory_space=pltpu.VMEM), pl.BlockSpec(memory_space=pl.ANY)),
         scratch_shapes=[
             pltpu.VMEM((1, clusters), F32),
@@ -206,15 +224,19 @@
             pltpu.SemaphoreType.DMA((2,)),
             pltpu.SemaphoreType.DMA((2,)),
         ],
-        compiler_params=pltpu.CompilerParams(collective_id=0, has_side_effects=True),
+        compiler_params=pltpu.CompilerParams(
+            collective_id=0, has_side_effects=True, vmem_limit_bytes=16 * 1024 * 1024
+        ),
         name="exchange",
-    )(charge, row, column, moment, owner, count, shaping)
+    )(*(in_hbm(x) for x in (charge, row, column, moment, owner, count, shaping)))
 
 
 def digitize_kernel(
-    row_count, bins, recv_ref, table_ref, response_ref, out_ref,
-    high, low, table, wides, hits, shaped, edges, held, staged, table_sem, out_sem,
+    row_count, bins, recv_ref, table_ref, weights_ref, out_ref,
+    high, high8, low8, table, table8, wides, wides8, hits, hits8, shaped, owns, edges, held, staged, response_ref, table_sem, weights_sem, out_sem,
 ):
+    fetch = pltpu.make_async_copy(weights_ref, response_ref, weights_sem)
+    fetch.start()
     load = pltpu.make_async_copy(table_ref, table, table_sem)
     load.start()
     slabs = recv_ref.shape[1]
@@ -237,49 +259,124 @@
             for slab in range(2)
         ]
 
-    def hit_rows(which, slab, slot):
-        at = HALF * slab + CAP * 3 + (slot % 2) * pairs + slot // 2
-        column = recv_ref[which, :, at : at + 1].astype(jnp.int32)
-        moment = lax.broadcasted_iota(jnp.int32, (slabs, bins), 1)
-        return jnp.where(moment == column, 1.0, 0.0).astype(BF16)
-
-    own = sides(1)
+    lane = lax.broadcasted_iota(jnp.int32, (slabs, LANES), 1).astype(F32)
+
+    def digits(which, slab):
+        at = HALF * slab + CAP * 3
+        moment = recv_ref[which, :, at : at + CAP]
+        block = jnp.floor(moment * (1.0 / LANES))
+        return block, moment - LANES * block
+
+    def hit_rows(digit, slot):
+        at = (slot % 2) * pairs + slot // 2
+        block, inner = (jnp.broadcast_to(d[:, at : at + 1], (slabs, LANES)) for d in digit)
+        row = jnp.where(inner == lane, 1.0, 0.0).astype(BF16)
+        block = block.astype(BF16)
+        zero = jnp.zeros((slabs, LANES), BF16)
+        return [jnp.where(block == float(k), row, zero) for k in range(bins // LANES)]
+
+    def keep(at, grid, to, width):
+        top = grid.astype(BF16)
+        there = pl.ds(at, grid.shape[0]), pl.ds(to, width)
+        high[there] = top
+        high8[there] = grid.astype(F8)
+        low8[there] = ((grid - top.astype(F32)) * GRID_LOW).astype(F8)
+
+    half_rows = row_count // 2
+    half_cells = half_rows * STRIDE
+    bases = (0, UPPER)
     pad = lax.broadcasted_iota(jnp.int32, (STRIDE, 2 * slabs), 0)
+    charges, rows_of, columns_of = [], [], []
+    place = 2 * lax.broadcasted_iota(jnp.int32, (pairs, 2 * slabs), 0) + (
+        lax.broadcasted_iota(jnp.int32, (pairs, 2 * slabs), 1) // slabs
+    )
+    spill = jnp.zeros((pairs, 2 * slabs), F32)
+    for fields in sides(1):
+        charge, row, column, _ = fields
+        charges.append(charge * GRID)
+        rows_of.append(row)
+        columns_of.append(column)
+        slab = len(charges) - 1
+        for index, field in enumerate((charges[-1], row, column)):
+            owns[slab, index] = field
+        outside = jnp.where(row < float(half_rows), CAP - MAIN - place, place - MAIN + 1)
+        spill = jnp.where(jnp.logical_and(charge != 0.0, outside > 0), 1.0, spill)
+
+    def fill(slab, half, which, lines_of):
+        for pair in which:
+            charge, row, column = lines_of(pair)
+            first = half_rows * half if isinstance(half, int) else (half_rows * half).astype(F32)
+            top = charge.astype(BF16).astype(F32)
+            rest = (charge - top) * CHARGE_LOW
+            lanes = pl.ds(pl.multiple_of(2 * slabs * pair, 2 * slabs), 2 * slabs)
+            for lead in range(0, half_rows, 4):
+                count = min(4, half_rows - lead)
+                size = count * STRIDE
+                pads = jnp.concatenate([pad] * count, axis=0).astype(F32).astype(BF16)
+                there = pads == jnp.broadcast_to(column, (size, 2 * slabs)).astype(BF16)
+                blank = jnp.zeros((size, 2 * slabs), BF16)
+                for part, target in ((top, wides), (rest, wides8)):
+                    lines = []
+                    for r in range(lead, lead + count):
+                        value = jnp.where(row == first + float(r), part, 0.0)
+                        lines.append(jnp.broadcast_to(value, (STRIDE, 2 * slabs)))
+                    values = jnp.concatenate(lines, axis=0).astype(BF16)
+                    target[slab, half, lead * STRIDE : lead * STRIDE + size, lanes] = jnp.where(
+                        there, values, blank
+                    ).astype(target.dtype)
+
+    def lay(slab, half, begin, end):
+        inner = slice(begin * slabs, end * slabs)
+        grid = jnp.dot(wides[slab, half, :, inner], hits[slab, inner], preferred_element_type=F32)
+        grid += (1.0 / CHARGE_LOW) * jnp.dot(
+            wides8[slab, half, :, inner], hits8[slab, inner], preferred_element_type=F32
+        )
+        base = bases[half] if isinstance(half, int) else pl.multiple_of(UPPER * half, UPPER)
+        to = bins * (1 - slab) if isinstance(slab, int) else pl.multiple_of(bins * (1 - slab), bins)
+        keep(base, grid, to, bins)
+
     for slab in range(2):
-        charge, row, column, _ = own[slab]
-        wide = wides.at[slab]
-        for pair in range(pairs):
-            there = pad == column[pair : pair + 1].astype(jnp.int32)
-            lanes = slice(2 * slabs * pair, 2 * slabs * (pair + 1))
-            for lead in range(0, row_count, 2):
-                both = []
-                for r in (lead, lead + 1):
-                    value = jnp.where(row[pair : pair + 1] == float(r), charge[pair : pair + 1], 0.0)
-                    both.append(jnp.where(there, value, 0.0))
-                top, rest = split(jnp.concatenate(both, axis=0))
-                at = lead * STRIDE
-                wide[at : at + 2 * STRIDE, lanes] = top
-                wide[cells + at : cells + at + 2 * STRIDE, lanes] = rest
+        digit = digits(1, slab)
         for slot in range(CAP):
-            hits[slab, slabs * slot : slabs * (slot + 1)] = hit_rows(1, slab, slot)
-        base = bins * (1 - slab)
-        both = jnp.dot(wide[...], hits[slab], preferred_element_type=F32)
-        top, rest = split(both[:cells] + both[cells:])
-        high[STRIDE : STRIDE + cells, base : base + bins] = top
-        low[STRIDE : STRIDE + cells, base : base + bins] = rest
+            for k, piece in enumerate(hit_rows(digit, slot)):
+                there = slice(slabs * slot, slabs * (slot + 1))
+                hits[slab, there, LANES * k : LANES * (k + 1)] = piece
+                hits8[slab, there, LANES * k : LANES * (k + 1)] = piece.astype(F8)
+        for half, begin in ((0, CAP - MAIN), (1, 0)):
+            fill(
+                slab,
+                half,
+                range(begin // 2, (begin + MAIN) // 2),
+                lambda pair: [f[slab][pair : pair + 1] for f in (charges, rows_of, columns_of)],
+            )
+            lay(slab, half, begin, begin + MAIN)
+
+    @pl.when(jnp.max(spill) > 0.0)
+    def _():
+        def again(index, carry):
+            slab, half = index // 2, index % 2
+            rest = (CAP - MAIN) // 2
+            pair = (pairs - rest) * half
+            fill(
+                slab,
+                half,
+                [pair + k for k in range(rest)],
+                lambda pair: [owns[slab, k, pl.ds(pair, 1)] for k in range(3)],
+            )
+            lay(slab, half, 0, CAP)
+            return carry
+
+        lax.fori_loop(0, 4, again, 0)
 
     held[...] = jnp.zeros(held.shape, F32)
     needed = jnp.zeros((), F32)
     for index, which in enumerate((0, 2)):
         fields = sides(which)
         edge = float(row_count - 1) if which == 0 else 0.0
-        place = 2 * lax.broadcasted_iota(jnp.int32, (pairs, 2 * slabs), 0) + (
-            lax.broadcasted_iota(jnp.int32, (pairs, 2 * slabs), 1) // slabs
-        )
         depth = (place if which == 0 else CAP - 1 - place) + 1
         for slab in range(2):
             charge, row, column, _ = fields[slab]
-            kept = jnp.where(row == edge, charge, 0.0)
+            kept = jnp.where(row == edge, charge * GRID, 0.0)
             needed = jnp.maximum(needed, jnp.max(jnp.where(kept != 0.0, depth, 0).astype(F32)))
             edges[index, slab, 0] = kept
             edges[index, slab, 1] = column
@@ -298,42 +395,49 @@
                     top = jnp.concatenate(weights, axis=1)
                     rest = top - top.astype(BF16).astype(F32)
                     left = jnp.concatenate([top, rest], axis=0).astype(BF16)
+                    digit = digits(which, slab)
                     right = jnp.concatenate(
-                        [hit_rows(which, slab, first + k) for k in range(4)], axis=0
+                        [jnp.concatenate(hit_rows(digit, first + k), axis=1) for k in range(4)], axis=0
                     )
                     both = jnp.dot(left, right, preferred_element_type=F32)
                     at = bins * (1 - slab)
                     held[index, :, at : at + bins] += both[:STRIDE] + both[STRIDE:]
 
-    for index, at in enumerate((0, STRIDE + cells)):
-        top, rest = split(held[index])
-        high[at : at + STRIDE] = top
-        low[at : at + STRIDE] = rest
+    for index in range(2):
+        keep(bases[index] + half_cells, held[index], 0, 2 * bins)
 
     load.wait()
+    table8[0] = (table[0].astype(F32) * TABLE_HIGH).astype(F8)
+    table8[1] = (table[1].astype(F32) * TABLE_LOW).astype(F8)
     depth = table.shape[1]
     steps = bins // TILE
+    fetch.wait()
+    weights = [[response_ref[a, b] * (1.0 / GRID) for b in range(3)] for a in range(3)]
     copies = []
     for step in range(steps + 1):
         if step < steps:
-            upper = high[:, TILE * step : TILE * step + depth]
-            shaped[step % 2] = (
-                jnp.dot(upper, table[0], preferred_element_type=F32)
-                + jnp.dot(upper, table[1], preferred_element_type=F32)
-                + jnp.dot(
-                    low[:, TILE * step : TILE * step + depth], table[0], preferred_element_type=F32
-                )
+            near = slice(TILE * step, TILE * step + depth)
+            fine = jnp.dot(
+                jnp.concatenate([low8[:, near], high8[:, near]], axis=1),
+                table8[...].reshape(2 * depth, TILE),
+                preferred_element_type=F32,
             )
+            shaped[step % 2] = jnp.dot(high[:, near], table[0], preferred_element_type=F32) + FINE * fine
         if step > 0:
             done = step - 1
             if done >= 2:
                 copies[done - 2].wait()
             for r in range(row_count):
-                near = [shaped[done % 2, STRIDE * (r + a) : STRIDE * (r + a + 1)] for a in range(3)]
+                near = []
+                for a in range(3):
+                    at = r + a - 1
+                    at = half_rows if at < 0 else at
+                    at = at * STRIDE if r + a <= half_rows else UPPER + (at - half_rows) * STRIDE
+                    near.append(shaped[done % 2, at : at + STRIDE])
                 sums = []
                 for b in range(3):
                     sums.append(
-                        response_ref[0, b] * near[0] + response_ref[1, b] * near[1] + response_ref[2, b] * near[2]
+                        weights[0][b] * near[0] + weights[1][b] * near[1] + weights[2][b] * near[2]
                     )
                 total = sums[1] + pltpu.roll(sums[0], 1, 0) + pltpu.roll(sums[2], STRIDE - 1, 0)
                 staged[done % 2, r] = total[:PPR]
@@ -352,32 +456,39 @@
 def digitize(recv, table, response, row_count, bins):
     slabs = recv.shape[1]
     cells = row_count * STRIDE
-    grid_rows = cells + 2 * STRIDE
+    grid_rows = UPPER + cells // 2 + STRIDE
     return pl.pallas_call(
         functools.partial(digitize_kernel, row_count, bins),
         out_shape=jax.ShapeDtypeStruct((row_count, PPR, bins), F32),
         in_specs=[
             pl.BlockSpec(memory_space=pltpu.VMEM),
             pl.BlockSpec(memory_space=pl.ANY),
-            pl.BlockSpec(memory_space=pltpu.SMEM),
+            pl.BlockSpec(memory_space=pltpu.HBM),
         ],
         out_specs=pl.BlockSpec(memory_space=pl.ANY),
         scratch_shapes=[
             pltpu.VMEM((grid_rows, 2 * bins), BF16),
-            pltpu.VMEM((grid_rows, 2 * bins), BF16),
+            pltpu.VMEM((grid_rows, 2 * bins), F8),
+            pltpu.VMEM((grid_rows, 2 * bins), F8),
             pltpu.VMEM(table.shape, BF16),
-            pltpu.VMEM((2, 2 * cells, CAP * slabs), BF16),
+            pltpu.VMEM(table.shape, F8),
+            pltpu.VMEM((2, 2, cells // 2, CAP * slabs), BF16),
+            pltpu.VMEM((2, 2, cells // 2, CAP * slabs), F8),
             pltpu.VMEM((2, CAP * slabs, bins), BF16),
+            pltpu.VMEM((2, CAP * slabs, bins), F8),
             pltpu.VMEM((2, grid_rows, TILE), F32),
+            pltpu.VMEM((2, 3, CAP // 2, 2 * slabs), F32),
             pltpu.VMEM((2, 2, 2, CAP // 2, 2 * slabs), F32),
             pltpu.VMEM((2, STRIDE, 2 * bins), F32),
             pltpu.VMEM((2, row_count, PPR, TILE), F32),
+            pltpu.SMEM(response.shape, F32),
+            pltpu.SemaphoreType.DMA,
             pltpu.SemaphoreType.DMA,
             pltpu.SemaphoreType.DMA((2,)),
         ],
-        compiler_params=pltpu.CompilerParams(vmem_limit_bytes=60 * 1024 * 1024),
+        compiler_params=pltpu.CompilerParams(vmem_limit_bytes=40 * 1024 * 1024),
         name="digitize",
-    )(recv, table, response)
+    )(recv, table, in_hbm(response))
 
 
 def solution(mesh):

time: 48 us -> 44.2 us (0.921)
  Pallas kernels: 47.7 us -> 44 us
    pallas_call x1, Pallas kernels: 19.1 us -> 16 us  [digitize(): pl.pallas_call(functools.partial(digitize_kernel, row_count, bins), out_s...]
    pallas_call x1, Pallas kernels: 28.6 us -> 27.9 us  [exchange(): pl.pallas_call(functools.partial(exchange_kernel, last_row, rows_y, slabs...]
where the time goes in v2:
time: 44.2 us; the launch traced here: 44.1 us
  Pallas kernels  44 us (100%)
    pallas_call x1, Pallas kernels, exchange(): pl.pallas_call(functools.partial(exchange_kernel, last_row, rows_y, slabs...  27.9 us
    pallas_call x1, Pallas kernels, digitize(): pl.pallas_call(functools.partial(digitize_kernel, row_count, bins), out_s...  16 us

profile of v2, /device:TPU:1, one launch (start us, length us, event | category | flops | bytes accessed | tf_op | source)
XLA Modules:
  0.0 44.1 jit_solution(4967408802795424831)
XLA Ops:
  0.0 27.9 %exchange.1 = (f32[3,64,128]{2,1,0:T(8,128)S(1)}, bf16[2,1280,256]{2,1,0:T(8,128)(2,1)S(1)}) custom-call(f32[1,512]{1,0:T(1,128)} %charge_ref.1, s32[1,512]{1,0:T(1,128)} %row_ref.1, s32[1,512]{1,0:T(1,128)} %column_ref.1, s32[1,512]{1,0:T(1,128)} %bin_ref.1, s32[1,512]{1,0:T(1,128)} %bitcast.3, s32[1,4]{1,0:T(1,128)} %count_ref.1, f32[1,1024]{1,0:T(1,128)} %bitcast.2), custom_call_target="tpu_custom_call" | custom-call | tf_op jit(solution)/shard_map/exchange/pallas_call | solution.py:206
  27.9 16.0 %digitize.1 = f32[10,66,1024]{2,1,0:T(8,128)} custom-call(f32[3,64,128]{2,1,0:T(8,128)S(1)} %get-tuple-element.7.recv_ref, bf16[2,1280,256]{2,1,0:T(8,128)(2,1)S(1)} %get-tuple-element.8.table_ref, f32[3,3]{1,0:T(4,128)} %weights_ref.1), custom_call_target="tpu_custom_call" | custom-call | tf_op jit(solution)/shard_map/digitize/pallas_call | solution.py:460

commit v3 on v1

v3 whole, which is shorter than its diff:
```python
import functools

import jax
import jax.numpy as jnp
from jax import lax
from jax.experimental import pallas as pl
from jax.experimental.pallas import tpu as pltpu
from jax.sharding import PartitionSpec as P

PROWS = 80
PPR = 66
STRIDE = 72
CAP = 16
FIELDS = 4
HALF = FIELDS * CAP
F32 = jnp.float32
BF16 = jnp.bfloat16
F8 = jnp.float8_e4m3fn
GRID, GRID_LOW = 2.0**-3, 2.0**8
TABLE_HIGH, TABLE_LOW = 2.0**7, 2.0**15
CHARGE_LOW = 2.0**17
FINE = 2.0**-15
LANES = 128
TILE = 256
NT = (((1,), (1,)), ((), ()))


def split(x):
    high = x.astype(BF16)
    return high, (x - high.astype(F32)).astype(BF16)


def route_rows(last_row, slabs, charge, row, column, moment, owner, count):
    clusters = charge.shape[1]
    lane = lax.broadcasted_iota(jnp.int32, (1, clusters), 1)
    limit = jnp.zeros((1, clusters), jnp.int32)
    for block in range(clusters // LANES):
        limit = jnp.where(lane // LANES == block, count[:, block : block + 1], limit)
    live = lane % LANES < limit
    owner = jnp.where(live, owner, slabs)
    mine = owner == lax.broadcasted_iota(jnp.int32, (slabs, clusters), 0)
    middle = (last_row + 1) // 2
    order = (
        row == last_row,
        jnp.logical_and(row >= middle, row < last_row),
        jnp.logical_and(row < middle, row > 0),
        row == 0,
    )
    kinds = [jnp.where(jnp.logical_and(mine, kind), 1.0, 0.0) for kind in order]
    stacked = jnp.concatenate(kinds, axis=0).astype(BF16)
    earlier = (
        lax.broadcasted_iota(jnp.int32, (clusters, clusters), 0)
        < lax.broadcasted_iota(jnp.int32, (clusters, clusters), 1)
    ).astype(F32).astype(BF16)
    ranks = jnp.dot(stacked, earlier, preferred_element_type=F32)
    ranks = [ranks[slabs * k : slabs * (k + 1)] for k in range(4)]
    firsts = jnp.sum(kinds[0], axis=1, keepdims=True)
    lasts = jnp.sum(kinds[3], axis=1, keepdims=True)
    places = (
        kinds[0] * ranks[0]
        + kinds[1] * (firsts + ranks[1])
        + kinds[2] * ((CAP - 1) - lasts - ranks[2])
        + kinds[3] * ((CAP - 1) - ranks[3])
    )
    place = jnp.sum(places, axis=0, keepdims=True)
    slot = lax.broadcasted_iota(jnp.int32, (CAP, clusters), 0)
    half = CAP // 2
    here = place == (2 * (slot % half) + slot // half).astype(F32)
    fields = (charge, row.astype(F32), column.astype(F32), moment.astype(F32))
    spread_out = jnp.concatenate([jnp.where(here, field, 0.0) for field in fields], axis=0)
    own = lax.dot_general(
        jnp.where(mine, 1.0, 0.0), spread_out, NT, precision=lax.Precision.HIGHEST, preferred_element_type=F32
    )
    slab = lax.broadcasted_iota(jnp.int32, own.shape, 0)
    before = jnp.where(slab == 0, 0.0, pltpu.roll(own, 1, 0))
    return jnp.concatenate([own, before], axis=1)


def lag_table(shaping):
    lags = shaping.shape[1]
    line = jnp.concatenate([jnp.zeros((1, TILE), F32), shaping, jnp.zeros((1, TILE), F32)], axis=1)
    rolled = pltpu.roll(
        jnp.broadcast_to(line, (TILE, lags + 2 * TILE)), 0, 1, stride=1, stride_axis=0
    )
    blocks = []
    for block in range(lags // TILE + 1):
        at = lags + TILE - TILE * block
        blocks.append(rolled[:, at : at + TILE])
    return blocks


def in_hbm(x):
    return pltpu.with_memory_space_constraint(x, pltpu.HBM)


def zigzag(step, size):
    half = (step + 1) // 2
    away = jnp.where(step % 2 == 0, half, -half)
    return lax.rem(size // 2 + away + size, size)


def exchange_kernel(
    last_row, rows_y, rows_z, charge_ref, row_ref, column_ref, bin_ref, owner_ref, count_ref, shaping_ref,
    out_ref, table_ref, floats, ints, counts, line, rows, table, load_sem, send_sem, recv_sem,
):
    slabs = rows.shape[0]
    me = lax.axis_index("tm")
    group = lax.axis_index("pad")
    my_y, my_z = me // rows_z, lax.rem(me, rows_z)
    loads = [
        pltpu.make_async_copy(source, target, load_sem.at[index])
        for index, (source, target) in enumerate(
            (
                (charge_ref, floats),
                (row_ref, ints.at[0]),
                (column_ref, ints.at[1]),
                (bin_ref, ints.at[2]),
                (owner_ref, ints.at[3]),
                (count_ref, counts),
                (shaping_ref, line),
            )
        )
    ]
    for load in loads:
        load.start()

    def peer_of(step):
        z = lax.rem(my_z + zigzag(step // rows_y, rows_z), rows_z)
        y = lax.rem(my_y + zigzag(lax.rem(step, rows_y), rows_y), rows_y)
        return y * rows_z + z

    barrier = pltpu.get_barrier_semaphore()

    def greet(step, carry):
        pl.semaphore_signal(
            barrier, inc=1, device_id=(peer_of(step), group), device_id_type=pl.DeviceIdType.MESH
        )
        return carry

    lax.fori_loop(0, slabs - 1, greet, 0)
    for load in loads:
        load.wait()
    rows[...] = route_rows(
        last_row, slabs, floats[...], ints[0], ints[1], ints[2], ints[3], counts[...]
    )
    for index, block in enumerate(lag_table(line[...])):
        high, low = split(block)
        table[0, TILE * index : TILE * (index + 1)] = high
        table[1, TILE * index : TILE * (index + 1)] = low
    store = pltpu.make_async_copy(table, table_ref, load_sem.at[0])
    store.start()
    out_ref[pl.ds(me, 1)] = rows[pl.ds(me, 1)]
    pl.semaphore_wait(barrier, slabs - 1)

    def send(step, carry):
        peer = peer_of(step)
        pltpu.make_async_remote_copy(
            src_ref=rows.at[pl.ds(peer, 1)],
            dst_ref=out_ref.at[pl.ds(me, 1)],
            send_sem=send_sem,
            recv_sem=recv_sem,
            device_id=(peer, group),
            device_id_type=pl.DeviceIdType.MESH,
        ).start()
        return carry

    lax.fori_loop(0, slabs - 1, send, 0)
    some = rows.at[pl.ds(0, slabs - 1)]
    there = out_ref.at[pl.ds(0, slabs - 1)]
    pltpu.make_async_copy(some, there, recv_sem).wait()
    pltpu.make_async_copy(some, there, send_sem).wait()
    store.wait()


def exchange(charge, row, column, moment, owner, count, shaping, slabs, last_row, rows_y):
    clusters, lags = charge.shape[1], shaping.shape[1]
    return pl.pallas_call(
        functools.partial(exchange_kernel, last_row, rows_y, slabs // rows_y),
        out_shape=(
            jax.ShapeDtypeStruct((slabs, 2 * HALF), F32),
            jax.ShapeDtypeStruct((2, lags + TILE, TILE), BF16),
        ),
        in_specs=[pl.BlockSpec(memory_space=pltpu.HBM)] * 7,
        out_specs=(pl.BlockSpec(memory_space=pltpu.VMEM), pl.BlockSpec(memory_space=pl.ANY)),
        scratch_shapes=[
            pltpu.VMEM((1, clusters), F32),
            pltpu.VMEM((4, 1, clusters), jnp.int32),
            pltpu.VMEM(count.shape, jnp.int32),
            pltpu.VMEM((1, lags), F32),
            pltpu.VMEM((slabs, 2 * HALF), F32),
            pltpu.VMEM((2, lags + TILE, TILE), BF16),
            pltpu.SemaphoreType.DMA((7,)),
            pltpu.SemaphoreType.DMA,
            pltpu.SemaphoreType.DMA,
        ],
        compiler_params=pltpu.CompilerParams(
            collective_id=0, has_side_effects=True, vmem_limit_bytes=16 * 1024 * 1024
        ),
        name="exchange",
    )(*(in_hbm(x) for x in (charge, row, column, moment, owner, count, shaping)))


def slot_fields(received):
    flipped = jnp.transpose(received)
    half = CAP // 2
    found = []
    for slab in range(2):
        found.append([])
        for field in range(FIELDS):
            at = HALF * slab + CAP * field
            found[-1].append(
                jnp.concatenate([flipped[at : at + half], flipped[at + half : at + CAP]], axis=1)
            )
    return found


def hit_rows(moments, slot, bins):
    slabs = moments.shape[0]
    lane = lax.broadcasted_iota(jnp.int32, (slabs, LANES), 1).astype(F32)
    at = (slot % 2) * (CAP // 2) + slot // 2
    block = jnp.floor(moments * (1.0 / LANES))
    block, inner = (
        jnp.broadcast_to(d[:, at : at + 1], (slabs, LANES)) for d in (block, moments - LANES * block)
    )
    row = jnp.where(inner == lane, 1.0, 0.0).astype(BF16)
    block = block.astype(BF16)
    zero = jnp.zeros((slabs, LANES), BF16)
    return [jnp.where(block == float(k), row, zero) for k in range(bins // LANES)]


def keep(refs, at, grid, to):
    top = grid.astype(BF16)
    rows, width = grid.shape
    refs[0][at : at + rows, to : to + width] = top
    refs[1][at : at + rows, to : to + width] = grid.astype(F8)
    refs[2][at : at + rows, to : to + width] = ((grid - top.astype(F32)) * GRID_LOW).astype(F8)


def deposit_kernel(
    row_count, bins, recv_ref, high, high8, low8, sides_ref, wides, wides8, hits, hits8, send_sem, recv_sem
):
    slabs = recv_ref.shape[0]
    groups = lax.axis_size("pad")
    me = lax.axis_index("tm")
    group = lax.axis_index("pad")
    above = lax.rem(group + 1, groups)
    below = lax.rem(group + groups - 1, groups)
    barrier = pltpu.get_barrier_semaphore()
    for side in (above, below):
        pl.semaphore_signal(barrier, inc=1, device_id=(me, side), device_id_type=pl.DeviceIdType.MESH)
    pairs = CAP // 2
    cells = row_count * STRIDE
    pad = lax.broadcasted_iota(jnp.int32, (STRIDE, 2 * slabs), 0)
    fields = slot_fields(recv_ref[...])
    copies = []
    for slab in range(2):
        charge, row, column, _ = fields[slab]
        charge = charge * GRID
        top = charge.astype(BF16).astype(F32)
        rest = (charge - top) * CHARGE_LOW
        for pair in range(pairs):
            lanes = slice(2 * slabs * pair, 2 * slabs * (pair + 1))
            for lead in range(0, row_count, 4):
                count = min(4, row_count - lead)
                size = count * STRIDE
                pads = jnp.concatenate([pad] * count, axis=0).astype(F32).astype(BF16)
                there = pads == jnp.broadcast_to(column[pair : pair + 1], (size, 2 * slabs)).astype(BF16)
                blank = jnp.zeros((size, 2 * slabs), BF16)
                for part, target in ((top, wides), (rest, wides8)):
                    lines = []
                    for r in range(lead, lead + count):
                        value = jnp.where(row[pair : pair + 1] == float(r), part[pair : pair + 1], 0.0)
                        lines.append(jnp.broadcast_to(value, (STRIDE, 2 * slabs)))
                    values = jnp.concatenate(lines, axis=0).astype(BF16)
                    target[slab, lead * STRIDE : lead * STRIDE + size, lanes] = jnp.where(
                        there, values, blank
                    ).astype(target.dtype)
        at = HALF * slab + CAP * 3
        moments = recv_ref[:, at : at + CAP]
        for slot in range(CAP):
            for k, piece in enumerate(hit_rows(moments, slot, bins)):
                there = slice(slabs * slot, slabs * (slot + 1))
                hits[slab, there, LANES * k : LANES * (k + 1)] = piece
                hits8[slab, there, LANES * k : LANES * (k + 1)] = piece.astype(F8)
        if slab == 0:
            pl.semaphore_wait(barrier, 2)
            for index, (side, place) in enumerate(((above, 0), (below, 1))):
                copies.append(
                    pltpu.make_async_remote_copy(
                        src_ref=recv_ref,
                        dst_ref=sides_ref.at[place],
                        send_sem=send_sem.at[index],
                        recv_sem=recv_sem.at[index],
                        device_id=(me, side),
                        device_id_type=pl.DeviceIdType.MESH,
                    )
                )
                copies[-1].start()
        grid = jnp.dot(wides[slab], hits[slab], preferred_element_type=F32)
        grid += (1.0 / CHARGE_LOW) * jnp.dot(wides8[slab], hits8[slab], preferred_element_type=F32)
        keep((high, high8, low8), 0, grid, bins * (1 - slab))
    for copy in copies:
        copy.wait()

    @pl.when(group == 0)
    def _():
        sides_ref[0] = jnp.zeros(sides_ref.shape[1:], F32)

    @pl.when(group == groups - 1)
    def _():
        sides_ref[1] = jnp.zeros(sides_ref.shape[1:], F32)


def deposit(recv, row_count, bins):
    slabs, width = recv.shape
    cells = row_count * STRIDE
    grid = (cells, 2 * bins)
    slots = CAP * slabs
    return pl.pallas_call(
        functools.partial(deposit_kernel, row_count, bins),
        out_shape=(
            jax.ShapeDtypeStruct(grid, BF16),
            jax.ShapeDtypeStruct(grid, F8),
            jax.ShapeDtypeStruct(grid, F8),
            jax.ShapeDtypeStruct((2, slabs, width), F32),
        ),
        in_specs=[pl.BlockSpec(memory_space=pltpu.VMEM)],
        out_specs=(pl.BlockSpec(memory_space=pltpu.VMEM),) * 4,
        scratch_shapes=[
            pltpu.VMEM((2, cells, slots), BF16),
            pltpu.VMEM((2, cells, slots), F8),
            pltpu.VMEM((2, slots, bins), BF16),
            pltpu.VMEM((2, slots, bins), F8),
            pltpu.SemaphoreType.DMA((2,)),
            pltpu.SemaphoreType.DMA((2,)),
        ],
        compiler_params=pltpu.CompilerParams(
            collective_id=1, has_side_effects=True, vmem_limit_bytes=36 * 1024 * 1024
        ),
        name="deposit",
    )(recv)


def shape_kernel(
    row_count, bins, high, high8, low8, sides_ref, table_ref, weights_ref, out_ref,
    edge_high, edge_high8, edge_low8, table, table8, shaped, edges, held, staged, response_ref,
    table_sem, weights_sem, out_sem,
):
    fetch = pltpu.make_async_copy(weights_ref, response_ref, weights_sem)
    fetch.start()
    load = pltpu.make_async_copy(table_ref, table, table_sem)
    load.start()
    slabs = sides_ref.shape[1]
    pairs = CAP // 2
    cells = row_count * STRIDE
    pad = lax.broadcasted_iota(jnp.int32, (STRIDE, 2 * slabs), 0)
    place = 2 * lax.broadcasted_iota(jnp.int32, (pairs, 2 * slabs), 0) + (
        lax.broadcasted_iota(jnp.int32, (pairs, 2 * slabs), 1) // slabs
    )
    held[...] = jnp.zeros(held.shape, F32)
    needed = jnp.zeros((), F32)
    for index in range(2):
        fields = slot_fields(sides_ref[index])
        edge = 0.0 if index else float(row_count - 1)
        depth = (CAP - 1 - place if index else place) + 1
        for slab in range(2):
            charge, row, column, _ = fields[slab]
            kept = jnp.where(row == edge, charge * GRID, 0.0)
            needed = jnp.maximum(needed, jnp.max(jnp.where(kept != 0.0, depth, 0).astype(F32)))
            edges[index, slab, 0] = kept
            edges[index, slab, 1] = column
    chunks = (needed.astype(jnp.int32) + 3) // 4
    for number in range(CAP // 4):

        @pl.when(number < chunks)
        def _():
            for index in range(2):
                first = CAP - 4 - 4 * number if index else 4 * number
                for slab in range(2):
                    weights = []
                    for pair in (first // 2, first // 2 + 1):
                        there = pad == edges[index, slab, 1, pair : pair + 1].astype(jnp.int32)
                        weights.append(jnp.where(there, edges[index, slab, 0, pair : pair + 1], 0.0))
                    top = jnp.concatenate(weights, axis=1)
                    rest = top - top.astype(BF16).astype(F32)
                    left = jnp.concatenate([top, rest], axis=0).astype(BF16)
                    at = HALF * slab + CAP * 3
                    moments = sides_ref[index, :, at : at + CAP]
                    right = jnp.concatenate(
                        [jnp.concatenate(hit_rows(moments, first + k, bins), axis=1) for k in range(4)], axis=0
                    )
                    both = jnp.dot(left, right, preferred_element_type=F32)
                    at = bins * (1 - slab)
                    held[index, :, at : at + bins] += both[:STRIDE] + both[STRIDE:]

    keep((edge_high, edge_high8, edge_low8), 0, held[...].reshape(2 * STRIDE, 2 * bins), 0)

    load.wait()
    table8[0] = (table[0].astype(F32) * TABLE_HIGH).astype(F8)
    table8[1] = (table[1].astype(F32) * TABLE_LOW).astype(F8)
    depth = table.shape[1]
    steps = bins // TILE
    fetch.wait()
    weights = [[response_ref[a, b] * (1.0 / GRID) for b in range(3)] for a in range(3)]
    copies = []
    for step in range(steps + 1):
        if step < steps:
            near = slice(TILE * step, TILE * step + depth)
            for at, rows, refs in (
                (0, cells, (high, high8, low8)),
                (cells, 2 * STRIDE, (edge_high, edge_high8, edge_low8)),
            ):
                fine = jnp.dot(
                    jnp.concatenate([refs[2][:, near], refs[1][:, near]], axis=1),
                    table8[...].reshape(2 * depth, TILE),
                    preferred_element_type=F32,
                )
                shaped[step % 2, at : at + rows] = (
                    jnp.dot(refs[0][:, near], table[0], preferred_element_type=F32) + FINE * fine
                )
        if step > 0:
            done = step - 1
            if done >= 2:
                copies[done - 2].wait()
            for r in range(row_count):
                near = []
                for a in range(3):
                    at = (r + a - 1) * STRIDE if 0 < r + a <= row_count else cells + STRIDE * (r + a > 0)
                    near.append(shaped[done % 2, at : at + STRIDE])
                sums = []
                for b in range(3):
                    sums.append(weights[0][b] * near[0] + weights[1][b] * near[1] + weights[2][b] * near[2])
                total = sums[1] + pltpu.roll(sums[0], 1, 0) + pltpu.roll(sums[2], STRIDE - 1, 0)
                staged[done % 2, r] = total[:PPR]
            copies.append(
                pltpu.make_async_copy(
                    staged.at[done % 2],
                    out_ref.at[:, :, pl.ds(TILE * done, TILE)],
                    out_sem.at[done % 2],
                )
            )
            copies[-1].start()
    for copy in copies[-2:]:
        copy.wait()


def shape_and_spread(high, high8, low8, sides, table, response, row_count, bins):
    slabs = sides.shape[1]
    edge = (2 * STRIDE, 2 * bins)
    vmem = pl.BlockSpec(memory_space=pltpu.VMEM)
    return pl.pallas_call(
        functools.partial(shape_kernel, row_count, bins),
        out_shape=jax.ShapeDtypeStruct((row_count, PPR, bins), F32),
        in_specs=[vmem, vmem, vmem, vmem, pl.BlockSpec(memory_space=pl.ANY), pl.BlockSpec(memory_space=pltpu.HBM)],
        out_specs=pl.BlockSpec(memory_space=pl.ANY),
        scratch_shapes=[
            pltpu.VMEM(edge, BF16),
            pltpu.VMEM(edge, F8),
            pltpu.VMEM(edge, F8),
            pltpu.VMEM(table.shape, BF16),
            pltpu.VMEM(table.shape, F8),
            pltpu.VMEM((2, row_count * STRIDE + 2 * STRIDE, TILE), F32),
            pltpu.VMEM((2, 2, 2, CAP // 2, 2 * slabs), F32),
            pltpu.VMEM((2, STRIDE, 2 * bins), F32),
            pltpu.VMEM((2, row_count, PPR, TILE), F32),
            pltpu.SMEM(response.shape, F32),
            pltpu.SemaphoreType.DMA,
            pltpu.SemaphoreType.DMA,
            pltpu.SemaphoreType.DMA((2,)),
        ],
        compiler_params=pltpu.CompilerParams(vmem_limit_bytes=36 * 1024 * 1024),
        name="shape",
    )(high, high8, low8, sides, table, in_hbm(response))


def solution(mesh):
    slabs, groups = mesh.shape["tm"], mesh.shape["pad"]
    row_count = PROWS // groups
    bins = 1024
    rows_y = 4 if slabs % 4 == 0 else 1

    def body(charge, pad_row, pad_column, time_bin, slab_owner, block_count, shaping, response):
        owner = slab_owner.reshape(1, slab_owner.shape[1])
        line = shaping.reshape(1, shaping.shape[0])
        received, table = exchange(
            charge, pad_row, pad_column, time_bin, owner, block_count, line, slabs, row_count - 1, rows_y
        )
        high, high8, low8, sides = deposit(received, row_count, bins)
        return shape_and_spread(high, high8, low8, sides, table, response, row_count, bins)

    in_specs = (P("pad", "tm"),) * 4 + (P("pad", "tm", None), P("pad", "tm"), P(), P())
    return jax.shard_map(
        body, mesh=mesh, in_specs=in_specs, out_specs=P("pad", None, "tm"), check_vma=False
    )
```

time: 48 us -> 44 us (0.917)
  Pallas kernels: 47.7 us -> 43.7 us
    pallas_call x1, Pallas kernels: 28.6 us -> 23.4 us  [exchange(): pl.pallas_call(functools.partial(exchange_kernel, last_row, rows_y, slabs...]
    pallas_call x1 -> x2, Pallas kernels: 19.1 us -> 20.3 us  [the longest x1 10.6 us: deposit(): pl.pallas_call(functools.partial(deposit_kernel, row_count, bins), out_sh...]
where the time goes in v3:
time: 44 us; the launch traced here: 43.9 us
  Pallas kernels  43.7 us (99%)
    pallas_call x1, Pallas kernels, exchange(): pl.pallas_call(functools.partial(exchange_kernel, last_row, rows_y, slabs...  23.4 us
    pallas_call x1, Pallas kernels, deposit(): pl.pallas_call(functools.partial(deposit_kernel, row_count, bins), out_sh...  10.6 us
    pallas_call x1, Pallas kernels, shape_and_spread(): pl.pallas_call(functools.partial(shape_kernel, row_count, bins), out_shap...  9.69 us

profile of v3, /device:TPU:1, one launch (start us, length us, event | category | flops | bytes accessed | tf_op | source)
XLA Modules:
  0.0 43.9 jit_solution(10468343682511043974)
XLA Ops:
  0.0 23.4 %exchange.1 = (f32[64,128]{1,0:T(8,128)S(1)}, bf16[2,1280,256]{2,1,0:T(8,128)(2,1)S(1)}) custom-call(f32[1,512]{1,0:T(1,128)} %charge_ref.1, s32[1,512]{1,0:T(1,128)} %row_ref.1, s32[1,512]{1,0:T(1,128)} %column_ref.1, s32[1,512]{1,0:T(1,128)} %bin_ref.1, s32[1,512]{1,0:T(1,128)} %bitcast.3, s32[1,4]{1,0:T(1,128)} %count_ref.1, f32[1,1024]{1,0:T(1,128)} %bitcast.2), custom_call_target="tpu_custom_call" | custom-call | tf_op jit(solution)/shard_map/exchange/pallas_call | solution.py:177
  23.4 10.6 %deposit.1 = (bf16[720,2048]{1,0:T(8,128)(2,1)S(1)}, f8e4m3fn[720,2048]{1,0:T(8,128)(4,1)S(1)}, f8e4m3fn[720,2048]{1,0:T(8,128)(4,1)S(1)}, f32[2,64,128]{2,1,0:T(8,128)S(1)}) custom-call(f32[64,128]{1,0:T(8,128)S(1)} %get-tuple-element.11.recv_ref), custom_call_target="tpu_custom_call" | custom-call | tf_op jit(solution)/shard_map/deposit/pallas_call | solution.py:319
  34.0 9.7 %shape.1 = f32[10,66,1024]{2,1,0:T(8,128)} custom-call(bf16[720,2048]{1,0:T(8,128)(2,1)S(1)} %get-tuple-element.12.high, f8e4m3fn[720,2048]{1,0:T(8,128)(4,1)S(1)} %get-tuple-element.13.high8, f8e4m3fn[720,2048]{1,0:T(8,128)(4,1)S(1)} %get-tuple-element.14.low8, f32[2,64,128]{2,1,0:T(8,128)S(1)} %get-tuple-element.15.sides_ref, ...), custom_call_target="tpu_custom_call" | custom-call | tf_op jit(solution)/shard_map/shape/pallas_call | solution.py:451

commit v4 on v3

--- a/solution.py
+++ b/solution.py
@@ -252,7 +252,7 @@
     cells = row_count * STRIDE
     pad = lax.broadcasted_iota(jnp.int32, (STRIDE, 2 * slabs), 0)
     fields = slot_fields(recv_ref[...])
-    copies = []
+    copies, grids = [], []
     for slab in range(2):
         charge, row, column, _ = fields[slab]
         charge = charge * GRID
@@ -282,7 +282,8 @@
                 there = slice(slabs * slot, slabs * (slot + 1))
                 hits[slab, there, LANES * k : LANES * (k + 1)] = piece
                 hits8[slab, there, LANES * k : LANES * (k + 1)] = piece.astype(F8)
-        if slab == 0:
+        if slab == 1:
+            keep((high, high8, low8), 0, grids[0], bins)
             pl.semaphore_wait(barrier, 2)
             for index, (side, place) in enumerate(((above, 0), (below, 1))):
                 copies.append(
@@ -298,7 +299,8 @@
                 copies[-1].start()
         grid = jnp.dot(wides[slab], hits[slab], preferred_element_type=F32)
         grid += (1.0 / CHARGE_LOW) * jnp.dot(wides8[slab], hits8[slab], preferred_element_type=F32)
-        keep((high, high8, low8), 0, grid, bins * (1 - slab))
+        grids.append(grid)
+    keep((high, high8, low8), 0, grids[1], 0)
     for copy in copies:
         copy.wait()
 
@@ -422,25 +424,27 @@
             done = step - 1
             if done >= 2:
                 copies[done - 2].wait()
-            for r in range(row_count):
-                near = []
-                for a in range(3):
-                    at = (r + a - 1) * STRIDE if 0 < r + a <= row_count else cells + STRIDE * (r + a > 0)
-                    near.append(shaped[done % 2, at : at + STRIDE])
-                sums = []
-                for b in range(3):
-                    sums.append(weights[0][b] * near[0] + weights[1][b] * near[1] + weights[2][b] * near[2])
-                total = sums[1] + pltpu.roll(sums[0], 1, 0) + pltpu.roll(sums[2], STRIDE - 1, 0)
-                staged[done % 2, r] = total[:PPR]
-            copies.append(
-                pltpu.make_async_copy(
-                    staged.at[done % 2],
-                    out_ref.at[:, :, pl.ds(TILE * done, TILE)],
-                    out_sem.at[done % 2],
+            parts = ((0, row_count),) if step < steps else ((0, row_count // 2), (row_count // 2, row_count))
+            for part, (begin, end) in enumerate(parts):
+                for r in range(begin, end):
+                    near = []
+                    for a in range(3):
+                        at = (r + a - 1) * STRIDE if 0 < r + a <= row_count else cells + STRIDE * (r + a > 0)
+                        near.append(shaped[done % 2, at : at + STRIDE])
+                    sums = []
+                    for b in range(3):
+                        sums.append(weights[0][b] * near[0] + weights[1][b] * near[1] + weights[2][b] * near[2])
+                    total = sums[1] + pltpu.roll(sums[0], 1, 0) + pltpu.roll(sums[2], STRIDE - 1, 0)
+                    staged[done % 2, r] = total[:PPR]
+                copies.append(
+                    pltpu.make_async_copy(
+                        staged.at[done % 2, pl.ds(begin, end - begin)],
+                        out_ref.at[pl.ds(begin, end - begin), :, pl.ds(TILE * done, TILE)],
+                        out_sem.at[2 if part else done % 2],
+                    )
                 )
-            )
-            copies[-1].start()
-    for copy in copies[-2:]:
+                copies[-1].start()
+    for copy in copies[-3:]:
         copy.wait()
 
 
@@ -466,7 +470,7 @@
             pltpu.SMEM(response.shape, F32),
             pltpu.SemaphoreType.DMA,
             pltpu.SemaphoreType.DMA,
-            pltpu.SemaphoreType.DMA((2,)),
+            pltpu.SemaphoreType.DMA((3,)),
         ],
         compiler_params=pltpu.CompilerParams(vmem_limit_bytes=36 * 1024 * 1024),
         name="shape",

time: 44 us -> 43.4 us (0.986)
  Pallas kernels: 43.7 us -> 43.1 us
    pallas_call x1, Pallas kernels: 10.6 us -> 10.1 us  [deposit(): pl.pallas_call(functools.partial(deposit_kernel, row_count, bins), out_sh...]
where the time goes in v4:
time: 43.4 us; the launch traced here: 43.2 us
  Pallas kernels  43.1 us (99%)
    pallas_call x1, Pallas kernels, exchange(): pl.pallas_call(functools.partial(exchange_kernel, last_row, rows_y, slabs...  23.4 us
    pallas_call x1, Pallas kernels, deposit(): pl.pallas_call(functools.partial(deposit_kernel, row_count, bins), out_sh...  10.1 us
    pallas_call x1, Pallas kernels, shape_and_spread(): pl.pallas_call(functools.partial(shape_kernel, row_count, bins), out_shap...  9.58 us

profile of v4, /device:TPU:1, one launch (start us, length us, event | category | flops | bytes accessed | tf_op | source)
XLA Modules:
  0.0 43.2 jit_solution(13505133990667000859)
XLA Ops:
  0.0 23.4 %exchange.1 = (f32[64,128]{1,0:T(8,128)S(1)}, bf16[2,1280,256]{2,1,0:T(8,128)(2,1)S(1)}) custom-call(f32[1,512]{1,0:T(1,128)} %charge_ref.1, s32[1,512]{1,0:T(1,128)} %row_ref.1, s32[1,512]{1,0:T(1,128)} %column_ref.1, s32[1,512]{1,0:T(1,128)} %bin_ref.1, s32[1,512]{1,0:T(1,128)} %bitcast.3, s32[1,4]{1,0:T(1,128)} %count_ref.1, f32[1,1024]{1,0:T(1,128)} %bitcast.2), custom_call_target="tpu_custom_call" | custom-call | tf_op jit(solution)/shard_map/exchange/pallas_call | solution.py:177
  23.4 10.1 %deposit.1 = (bf16[720,2048]{1,0:T(8,128)(2,1)S(1)}, f8e4m3fn[720,2048]{1,0:T(8,128)(4,1)S(1)}, f8e4m3fn[720,2048]{1,0:T(8,128)(4,1)S(1)}, f32[2,64,128]{2,1,0:T(8,128)S(1)}) custom-call(f32[64,128]{1,0:T(8,128)S(1)} %get-tuple-element.11.recv_ref), custom_call_target="tpu_custom_call" | custom-call | tf_op jit(solution)/shard_map/deposit/pallas_call | solution.py:321
  33.5 9.6 %shape.1 = f32[10,66,1024]{2,1,0:T(8,128)} custom-call(bf16[720,2048]{1,0:T(8,128)(2,1)S(1)} %get-tuple-element.12.high, f8e4m3fn[720,2048]{1,0:T(8,128)(4,1)S(1)} %get-tuple-element.13.high8, f8e4m3fn[720,2048]{1,0:T(8,128)(4,1)S(1)} %get-tuple-element.14.low8, f32[2,64,128]{2,1,0:T(8,128)S(1)} %get-tuple-element.15.sides_ref, ...), custom_call_target="tpu_custom_call" | custom-call | tf_op jit(solution)/shard_map/shape/pallas_call | solution.py:455
